TPU v7x, 32 devices: a whole 2x2x4 slice. The times are simulated.
32 devices in a mesh: seq: 8 (over y, x, core), batch: 4 (over z).
Axes of the slice: x: 2, y: 2, z: 4, core: 2. Of those that a mesh axis runs over, the one named last changes fastest.
Arguments:
- queries: bfloat16 [16, 4096], P('batch', 'seq'), may hold values from -210 to 210
- key_cache: bfloat16 [16, 1024, 2048], P('batch', 'seq'), may hold values from -6 to 6
- value_cache: bfloat16 [16, 1024, 2048], P('batch', 'seq'), may hold values from -12 to 12
- new_key: bfloat16 [16, 2048], P('batch'), may hold values from -6 to 6
- new_value: bfloat16 [16, 2048], P('batch'), may hold values from -12 to 12
- page_table: int32 [16, 8], P('batch', 'seq'), may hold values from 0 to 3, as said below
- counts: int32 [16, 8], P('batch', 'seq'), may hold values from 1 to 128
- offsets: int32 [16], P('batch'), may hold values from 0 to 896
- w_out: bfloat16 [4096, 4608], P('seq', 'batch'), may hold values from -0.09375 to 0.09375
Outputs:
- projected: bfloat16 [16, 4608], P('seq', 'batch')
Inputs may be any that keep to these rules, and one draw needn't show every extreme that they name: `page_table`: for each group of 4 requests and each index along seq, the slots of that index's 1 pages of the group's requests are all different.
All inputs are finite; a program needn't handle non-finite values.
Results may differ from a plain program's by a relative error of at most 0.005.
Values may be sent and summed in bfloat16 or wider, within the bound.
A program may use at most 64 MiB of HBM per device.

v0:
```python
import jax
import jax.numpy as jnp
from jax import lax
from jax.sharding import PartitionSpec as P

HEADS = 32
KVH = 16
HD = 128
QSCALAR = 144


floor_score = -1e30


def joined(x, axis, combine):
    everything = jax.tree.map(lambda part: lax.all_gather(part, axis), x)
    initial = jax.tree.map(lambda part: part[0], everything)

    def turn(k, so_far):
        return combine(so_far, jax.tree.map(lambda part: part[k], everything))

    return lax.fori_loop(1, lax.axis_size(axis), turn, initial)


def on_device(
    queries, key_cache, value_cache, new_key, new_value, page_table, counts, offsets, w_out
):
    requests = queries.shape[0]
    groups = HEADS // KVH
    cycle_size = lax.axis_size("seq")
    cycle_place = lax.axis_index("seq")
    head_count = HEADS // cycle_size
    pages_here = page_table.shape[1]
    page_len = key_cache.shape[1]
    score_multiplier = QSCALAR ** (-0.5)

    def own_heads(array_in):
        return lax.dynamic_slice_in_dim(array_in, cycle_place * head_count, head_count, 1)

    all_queries = lax.all_gather(queries, "seq", axis=1, tiled=True)
    query_lattice = all_queries.reshape(requests, KVH, groups, HD)
    key_rows = jnp.take(key_cache, page_table, axis=0).reshape(
        requests, pages_here * page_len, KVH, HD
    )
    value_rows = jnp.take(value_cache, page_table, axis=0).reshape(
        requests, pages_here * page_len, KVH, HD
    )
    scores = (
        jnp.einsum("bkgd,btkd->bkgt", query_lattice, key_rows, preferred_element_type=jnp.float32)
        * score_multiplier
    )
    token_index = jnp.arange(page_len, dtype=jnp.int32)
    page_start = (cycle_place * pages_here + jnp.arange(pages_here, dtype=jnp.int32)) * page_len
    live_mask = (token_index[None, None, :] < counts[:, :, None]) & (
        page_start[None, :, None] + token_index[None, None, :] >= offsets[:, None, None]
    )
    live_mask = live_mask.reshape(requests, pages_here * page_len)[:, None, None, :]
    peak_score = jnp.max(jnp.where(live_mask, scores, floor_score), axis=-1)
    weights = jnp.where(live_mask, jnp.exp(scores - peak_score[..., None]), 0.0)
    block_total = jnp.sum(weights, axis=-1)
    block_sum = jnp.einsum(
        "bkgt,btkd->bkgd",
        weights.astype(jnp.bfloat16),
        value_rows,
        preferred_element_type=jnp.float32,
    )
    incoming_score = (
        jnp.einsum(
            "pcoz,pcz->pco",
            query_lattice,
            new_key.reshape(requests, KVH, HD),
            preferred_element_type=jnp.float32,
        )
        * score_multiplier
    )
    fresh_value = jnp.broadcast_to(
        new_value.astype(jnp.float32).reshape(requests, KVH, 1, HD), (requests, KVH, groups, HD)
    ).reshape(requests, HEADS, HD)
    flat_peak = peak_score.reshape(requests, HEADS)
    flat_total = block_total.reshape(requests, HEADS)
    flat_sum = block_sum.reshape(requests, HEADS, HD)
    flat_new = incoming_score.reshape(requests, HEADS)
    mine_new = own_heads(flat_new)
    mine_value = own_heads(fresh_value)

    def combine(earlier, later):
        top_score = jnp.maximum(earlier[0], later[0])
        left_weight = jnp.exp(earlier[0] - top_score)
        trailing_weight = jnp.exp(later[0] - top_score)
        return (
            top_score,
            earlier[1] * left_weight + later[1] * trailing_weight,
            earlier[2] * left_weight[..., None] + later[2] * trailing_weight[..., None],
        )

    merged_peak, merged_total, merged_sum = joined(
        (flat_peak, flat_total, flat_sum), "seq", combine
    )
    head_peak = own_heads(merged_peak)
    top_score = jnp.maximum(head_peak, mine_new)
    factor = jnp.exp(head_peak - top_score)
    own_weight = jnp.exp(mine_new - top_score)
    denominator = own_heads(merged_total) * factor + own_weight
    numerator = own_heads(merged_sum) * factor[..., None] + own_weight[..., None] * mine_value
    attention = (
        (numerator / denominator[..., None]).astype(jnp.bfloat16).reshape(requests, head_count * HD)
    )
    everyone = lax.all_gather(attention, "batch", axis=0, tiled=True)
    projected = lax.psum_scatter(
        jnp.dot(everyone, w_out, preferred_element_type=jnp.float32),
        "seq",
        scatter_dimension=0,
        tiled=True,
    )
    return projected.astype(jnp.bfloat16)


def solution(mesh):
    placed = (
        P("batch", "seq"),
        P("batch", "seq", None),
        P("batch", "seq", None),
        P("batch", None),
        P("batch", None),
        P("batch", "seq"),
        P("batch", "seq"),
        P("batch"),
        P("seq", "batch"),
    )
    return jax.shard_map(
        on_device, mesh=mesh, in_specs=placed, out_specs=P("seq", "batch"), check_vma=False
    )
```

profile of v0, /device:TPU:0, one launch (start us, length us, event | category | flops | bytes accessed | tf_op | source)
XLA Modules:
  0.0 98.0 jit_solution(6286090056575001631)
XLA Ops:
  0.0 0.8 fusion.15
  0.8 0.8 copy-done
  1.6 2.0 %gather_fusion = bf16[4,128,2048]{2,1,0:T(8,128)(2,1)} fusion(bf16[4,128,2048]{2,1,0:T(8,128)(2,1)S(1)} %copy-done, s32[1024]{0:T(1024)S(1)} %pad_clamp_fusion), kind=kCustom, calls=%fused_computation.clone | custom fusion | bytes 4194320 | tf_op jit(solution)/shard_map/jit(_take)/gather | solution.py:42
  3.6 3.6 %gather_fusion.1 = bf16[4,128,2048]{2,1,0:T(8,128)(2,1)} fusion(bf16[4,128,2048]{2,1,0:T(8,128)(2,1)} %param.15, s32[1024]{0:T(1024)S(1)} %pad_clamp_fusion), kind=kCustom, calls=%fused_computation.1.clone | custom fusion | bytes 4194320 | tf_op jit(solution)/shard_map/jit(_take)/gather | solution.py:45
  7.2 4.0 %bitcast_select_fusion = (bf16[4,1,128,2048]{3,2,0,1:T(8,128)(2,1)}, bf16[4,1,128,2048]{3,2,0,1:T(8,128)(2,1)S(1)}) fusion(bf16[4,128,2048]{2,1,0:T(8,128)(2,1)} %gather_fusion.1, pred[4]{0:T(512)(128)(4,1)S(1)} %and_bitcast_fusion, bf16[4,128,2048]{2,1,0:T(8,128)(2,1)} %gather_fusion), kind=kLoop, calls=%fused_computation.10 | loop fusion | flops 2097152 | bytes 8388612 | tf_op jit(solution)/shard_map/jit(_take)/select_n | solution.py:45
  11.2 2.0 %copy.35 = bf16[64,8,16,128]{3,2,1,0:T(8,128)(2,1)} copy(bf16[64,8,16,128]{3,1,2,0:T(8,128)(2,1)S(1)} %bitcast.71) | data formatting | bytes 4194304
  13.3 10.6 %all_gather.15 = bf16[4,4096]{1,0:T(4,128)(2,1)S(1)} all-gather(bf16[4,512]{1,0:T(4,128)(2,1)S(1)} %copy-done.4), channel_id=1, replica_groups=mesh['seq'=8,'batch'=4] {'seq'}, dimensions={1}, use_global_device_ids=true | all-gather | bytes 36864 | tf_op jit(solution)/shard_map/all_gather | solution.py:40
  23.9 3.0 %select_reduce_fusion = (f32[4,16,2]{2,1,0:T(8,128)S(1)}, f32[4,16,128,2]{2,3,1,0:T(2,128)S(1)}) fusion(pred[4,128]{1,0:T(4,128)(4,1)S(1)} %fusion.13, bf16[4,16,2,128]{3,2,1,0:T(2,128)(2,1)S(1)} %reshape.104, bf16[4,128,16,128]{3,2,1,0:T(8,128)(2,1)} %bitcast.72), kind=kOutput, calls=%fused_computation.21 | convolution fusion | flops 4243328 | bytes 2196480 | tf_op jit(solution)/shard_map/bkgd,btkd->bkgt/dot_general | solution.py:49
  26.9 0.6 copy.36
  27.6 0.7 fusion.3
  28.3 9.8 %all_gather.18 = f32[8,4,32,128]{3,2,1,0:T(8,128)S(1)} all-gather(f32[1,4,32,128]{3,2,1,0:T(8,128)S(1)} %bitcast.76), channel_id=1, replica_groups=mesh['seq'=8,'batch'=4] {'seq'}, dimensions={0}, use_global_device_ids=true | all-gather | bytes 589824 | tf_op jit(solution)/shard_map/all_gather | solution.py:16
  38.1 0.3 bitcast_reduce_fusion
  38.4 0.2 copy.25
  38.7 7.9 %all_gather.17 = f32[8,4,32]{2,1,0:T(4,128)S(1)} all-gather(f32[1,4,32]{2,1,0:T(4,128)S(1)} %copy.26), channel_id=1, replica_groups=mesh['seq'=8,'batch'=4] {'seq'}, dimensions={0}, use_global_device_ids=true | all-gather | bytes 4608 | tf_op jit(solution)/shard_map/all_gather | solution.py:16
  46.6 0.2 copy.23
  46.9 8.9 %all_gather.16 = f32[8,4,32]{2,1,0:T(4,128)S(1)} all-gather(f32[1,4,32]{2,1,0:T(4,128)S(1)} %copy.24), channel_id=1, replica_groups=mesh['seq'=8,'batch'=4] {'seq'}, dimensions={0}, use_global_device_ids=true | all-gather | bytes 4608 | tf_op jit(solution)/shard_map/all_gather | solution.py:16
  55.8 1.1 %while.19 = (s32[]{:T(128)}, f32[4,32]{1,0:T(4,128)S(1)}, f32[4,32]{1,0:T(4,128)S(1)}, f32[4,32,128]{2,1,0:T(8,128)S(1)}, f32[8,4,32]{2,1,0:T(4,128)S(1)}, /*ind...) while((s32[]{:T(128)}, f32[4,32]{1,0:T(4,128)S(1)}, ...), condition=%wide.region_3.5_spmd, body=%wide.region_2.4_spmd.sunk | while | flops 49925 | bytes 201879 | solution.py:22
  55.8 0.1 fusion.29
  56.0 0.1 fusion.29
  56.1 0.1 fusion.29
  56.3 0.1 fusion.29
  56.5 0.1 fusion.29
  56.6 0.1 fusion.29
  56.8 0.1 fusion.29
  57.1 0.2 fusion.19
  57.3 0.2 copy.34
  57.6 0.1 copy.29
  58.0 13.4 %all-gather = bf16[4,4,512]{2,1,0:T(4,128)(2,1)S(1)} all-gather(bf16[1,4,512]{2,1,0:T(4,128)(2,1)S(1)} %reshape.129), channel_id=1, replica_groups=mesh['seq'=8,'batch'=4] {'batch'}, dimensions={0}, use_global_device_ids=true | all-gather | bytes 20480 | tf_op jit(solution)/shard_map/all_gather | solution.py:108
  71.5 1.5 %fusion.20 = f32[16,1152]{1,0:T(8,128)S(1)} fusion(bf16[16,512]{1,0:T(8,128)(2,1)S(1)} %reshape.130, bf16[512,1152]{1,0:T(8,128)(2,1)} %param.21), kind=kOutput, calls=%fused_computation.44 | convolution fusion | flops 18874368 | bytes 1269760 | tf_op jit(solution)/shard_map/dot_general | solution.py:110
  73.0 23.1 %all-reduce = bf16[16,1152]{1,0:T(8,128)(2,1)S(1)} all-reduce(f32[16,1152]{1,0:T(8,128)S(1)} %fusion.20), channel_id=2, replica_groups=mesh['seq'=8,'batch'=4] {'seq'}, use_global_device_ids=true, to_apply=%region_4.6.clone | all-reduce | flops 18432 | bytes 110592
  96.1 0.6 dynamic-slice
  97.4 0.6 dynamic-slice_convert_fusion
  (47 shorter events, 1.1 us)
Async XLA Ops:
  0.0 1.6 %copy-start = (bf16[4,128,2048]{2,1,0:T(8,128)(2,1)S(1)}, bf16[4,128,2048]{2,1,0:T(8,128)(2,1)}, u32[]{:S(2)}) copy-start(bf16[4,128,2048]{2,1,0:T(8,128)(2,1)} %param.14) | copy-start | bytes 6291460
  3.6 3.6 %copy-start.7 = (s32[4,1]{0,1:T(1,128)S(1)}, s32[4,1]{0,1:T(1,128)}, u32[]{:S(2)}) copy-start(s32[4,1]{0,1:T(1,128)} %param.18) | copy-start | bytes 52
  11.2 2.0 %copy-start.5 = (s32[4,1]{0,1:T(1,128)S(1)}, s32[4,1]{0,1:T(1,128)}, u32[]{:S(2)}) copy-start(s32[4,1]{0,1:T(1,128)} %param.19) | copy-start | bytes 52
  11.2 2.0 %copy-start.6 = (s32[4]{0:T(128)S(1)}, s32[4]{0:T(128)}, u32[]{:S(2)}) copy-start(s32[4]{0:T(128)} %param.20) | copy-start | bytes 52
  11.2 2.1 %copy-start.4 = (bf16[4,512]{1,0:T(4,128)(2,1)S(1)}, bf16[4,512]{1,0:T(4,128)(2,1)}, u32[]{:S(2)}) copy-start(bf16[4,512]{1,0:T(4,128)(2,1)} %param.13) | copy-start | bytes 12292
  23.9 3.0 %copy-start.1 = (bf16[4,1,128,2048]{3,2,0,1:T(8,128)(2,1)S(1)}, bf16[4,1,128,2048]{3,2,0,1:T(8,128)(2,1)}, u32[]{:S(2)}) copy-start(bf16[4,1,128,2048]{3,2,0,1:T(8,128)(2,1)} %get-tuple-element.215) | copy-start | bytes 6291460
  27.5 29.5 %copy-start.2 = (bf16[4,2048]{1,0:T(4,128)(2,1)S(1)}, bf16[4,2048]{1,0:T(4,128)(2,1)}, u32[]{:S(2)}) copy-start(bf16[4,2048]{1,0:T(4,128)(2,1)} %param.16) | copy-start | bytes 49156
  27.6 30.3 %copy-start.3 = (bf16[4,2048]{1,0:T(4,128)(2,1)S(1)}, bf16[4,2048]{1,0:T(4,128)(2,1)}, u32[]{:S(2)}) copy-start(bf16[4,2048]{1,0:T(4,128)(2,1)} %param.17) | copy-start | bytes 49156
  38.1 58.0 %copy-start.8 = (u32[32]{0:T(128)S(1)}, u32[32]{0:T(128)}, u32[]{:S(2)}) copy-start(u32[32]{0:T(128)} %constant.74) | copy-start | bytes 388
where the time goes:
time: 98.3 us; the launch traced here: 98 us
  blocking collectives  73.8 us (75%)
  local copies, waits for them, and re-layouts  11.6 us (12%)
  other arithmetic  6.21 us (6%)
  matrix products  5.44 us (6%)
    all_gather x3, blocking collectives, joined(): everything = jax.tree.map(lambda part: lax.all_gather(part, axis), x)  26.6 us
    unnamed x1, blocking collectives  23.1 us
    all_gather x1, blocking collectives, on_device(): everyone = lax.all_gather(attention, 'batch', axis=0, tiled=True)  13.4 us
    all_gather x1, blocking collectives, on_device(): all_queries = lax.all_gather(queries, 'seq', axis=1, tiled=True)  10.6 us
    unnamed x24, local copies, waits for them, and re-layouts  4.04 us
    select_n x1, other arithmetic, on_device(): jnp.take(value_cache, page_table, axis=0)  3.96 us
    gather x1, local copies, waits for them, and re-layouts, on_device(): jnp.take(value_cache, page_table, axis=0)  3.58 us
    dot_general x1, matrix products, on_device(): jnp.einsum('bkgd,btkd->bkgt', query_lattice, key_rows, preferred_element_...  3.01 us

commit v1 on v0

v1 whole, which is shorter than its diff:
```python
import functools

import jax
import jax.numpy as jnp
from jax import lax
from jax.experimental import pallas as pl
from jax.experimental.pallas import tpu as pltpu
from jax.sharding import PartitionSpec as P

HEADS = 32
KVH = 16
HD = 128
QSCALAR = 144
CHUNK = 2

floor_score = -1e30


def kernel(
    n,
    nb,
    q_hbm,
    k_hbm,
    v_hbm,
    nk_hbm,
    nv_hbm,
    table,
    counts,
    offsets,
    w_hbm,
    out_ref,
    q_all,
    k_ref,
    v_ref,
    nk_ref,
    nv_ref,
    w_ref,
    stat_send,
    stat_recv,
    sum_send,
    sum_recv,
    att_all,
    proj_send,
    proj_recv,
    load_sem,
    q_ss,
    q_rs,
    stat_ss,
    stat_rs,
    sum_ss,
    sum_rs,
    att_ss,
    att_rs,
    proj_ss,
    proj_rs,
):
    me = lax.axis_index("seq")
    mine = lax.axis_index("batch")
    requests = q_hbm.shape[0]
    slots, page_len, _ = k_hbm.shape
    pages = table.shape[1]
    tokens = slots * page_len
    groups = HEADS // KVH
    own = HEADS // n
    width = CHUNK * HD
    chunk_heads = CHUNK * groups
    rows = chunk_heads * requests
    n_chunks = KVH // CHUNK
    scale = QSCALAR ** (-0.5)
    f32 = jnp.float32

    loads = [
        pltpu.make_async_copy(src, dst, load_sem.at[i])
        for i, (src, dst) in enumerate(
            (
                (q_hbm, q_all.at[me]),
                (k_hbm, k_ref),
                (v_hbm, v_ref),
                (nk_hbm, nk_ref),
                (nv_hbm, nv_ref),
                (w_hbm, w_ref),
            )
        )
    ]
    for load in loads:
        load.start()

    barrier = pltpu.get_barrier_semaphore()
    for i in range(1, n):
        pl.semaphore_signal(barrier, inc=1, device_id={"seq": lax.rem(me + i, n)})
    for i in range(1, nb):
        pl.semaphore_signal(barrier, inc=1, device_id={"batch": lax.rem(mine + i, nb)})
    pl.semaphore_wait(barrier, n - 1 + nb - 1)

    def push(src, dst, ss, rs, axis, place, to):
        return pltpu.make_async_remote_copy(
            src_ref=src,
            dst_ref=dst,
            send_sem=ss.at[to],
            recv_sem=rs.at[place],
            device_id={axis: to},
        )

    for i in range(1, n):
        push(q_hbm, q_all.at[me], q_ss, q_rs, "seq", me, lax.rem(me + i, n)).start()

    row_request = lax.broadcasted_iota(jnp.int32, (rows, tokens), 0) % requests
    column = lax.broadcasted_iota(jnp.int32, (rows, tokens), 1)
    slot, token = column // page_len, column % page_len
    live = jnp.zeros((rows, tokens), jnp.bool_)
    first = jnp.zeros((rows, tokens), jnp.int32)
    for r in range(requests):
        first = jnp.where(row_request == r, offsets[r], first)
    for p in range(pages):
        where_at = jnp.zeros((rows, tokens), jnp.int32)
        count = jnp.zeros((rows, tokens), jnp.int32)
        for r in range(requests):
            where_at = jnp.where(row_request == r, table[r, p], where_at)
            count = jnp.where(row_request == r, counts[r, p], count)
        start = (me * pages + p) * page_len
        live = live | ((where_at == slot) & (token < count) & (start + token >= first))

    row = lax.broadcasted_iota(jnp.int32, (rows, HD), 0)
    lane = lax.broadcasted_iota(jnp.int32, (rows, HD), 1)

    def head_rows(ref, lead, head):
        at = pl.ds(pl.multiple_of(head * HD, HD), HD)
        return (ref[lead, :, at] if lead is not None else ref[:, at]).astype(f32)

    for load in loads[:3]:
        load.wait()
    for i in range(1, n):
        to = lax.rem(me + i, n)
        push(q_hbm, q_all.at[to], q_ss, q_rs, "seq", to, to).wait_recv()

    base = (me * own) // chunk_heads
    span = min(own, chunk_heads)
    for i in range(n_chunks):
        c = lax.rem(base + 1 + i, n_chunks)
        at = pl.ds(pl.multiple_of(c * width, width), width)
        head0 = c * chunk_heads
        parts = []
        for h in range(chunk_heads):
            parts.append(head_rows(q_all, (head0 + h) // own, (head0 + h) % own))
        q = jnp.concatenate(parts, axis=0)
        wide = jnp.concatenate(
            [
                jnp.where(row // (groups * requests) == k, q, 0.0).astype(jnp.bfloat16)
                for k in range(CHUNK)
            ],
            axis=1,
        )
        keys = k_ref[:, :, at].reshape(tokens, width)
        scores = (
            lax.dot_general(wide, keys, (((1,), (1,)), ((), ())), preferred_element_type=f32)
            * scale
        )
        peak = jnp.max(jnp.where(live, scores, floor_score), axis=1, keepdims=True)
        weights = jnp.where(live, jnp.exp(scores - peak), 0.0)
        total = jnp.sum(weights, axis=1, keepdims=True)
        values = v_ref[:, :, at].reshape(tokens, width)
        full = jnp.dot(weights.astype(jnp.bfloat16), values, preferred_element_type=f32)
        sums = jnp.concatenate(
            [
                full[k * groups * requests : (k + 1) * groups * requests, k * HD : (k + 1) * HD]
                for k in range(CHUNK)
            ],
            axis=0,
        )
        for part in range(chunk_heads // span):
            to = (head0 + part * span) // own
            height = span * requests
            low = part * height
            low_to = pl.multiple_of(((head0 + part * span) % own) * requests, requests)
            if own == span:
                low_to = 0
            hit = (row - low + low_to == lane) & (row >= low) & (row < low + height)
            stat = jnp.concatenate(
                [
                    jnp.sum(jnp.where(hit, peak, 0.0), axis=0, keepdims=True),
                    jnp.sum(jnp.where(hit, total, 0.0), axis=0, keepdims=True),
                ],
                axis=0,
            )
            stat_send[to] = stat
            sum_send[to] = sums[low : low + height].astype(sum_send.dtype)

            @pl.when(to != me)
            def _():
                push(stat_send.at[to], stat_recv.at[me], stat_ss, stat_rs, "seq", me, to).start()
                push(sum_send.at[to], sum_recv.at[me], sum_ss, sum_rs, "seq", me, to).start()

    own_rows = own * requests
    for load in loads[3:]:
        load.wait()
    kv = [(me * own + h) // groups for h in range(own)]
    own_q = jnp.concatenate([head_rows(q_all, me, h) for h in range(own)], axis=0)
    own_key = jnp.concatenate([head_rows(nk_ref, None, k) for k in kv], axis=0)
    own_value = jnp.concatenate([head_rows(nv_ref, None, k) for k in kv], axis=0)
    new_score = jnp.sum(own_q * own_key, axis=1, keepdims=True) * scale

    o_row = lax.broadcasted_iota(jnp.int32, (own_rows, HD), 0)
    o_lane = lax.broadcasted_iota(jnp.int32, (own_rows, HD), 1)
    diagonal = o_row == o_lane

    def to_column(line):
        return jnp.sum(jnp.where(diagonal, line, 0.0), axis=1, keepdims=True)

    for i in range(1, n):
        to = lax.rem(me + i, n)
        push(stat_send.at[to], stat_recv.at[to], stat_ss, stat_rs, "seq", to, to).wait_recv()
    stats = [stat_send[me]] + [stat_recv[lax.rem(me + i, n)] for i in range(1, n)]
    peaks = [to_column(s[0:1]) for s in stats]
    totals = [to_column(s[1:2]) for s in stats]
    top = new_score
    for peak in peaks:
        top = jnp.maximum(top, peak)
    own_weight = jnp.exp(new_score - top)
    factors = [jnp.exp(peak - top) for peak in peaks]
    denominator = own_weight
    for total, factor in zip(totals, factors):
        denominator = denominator + total * factor
    numerator = own_weight * own_value + factors[0] * sum_send[me].astype(f32)
    for i in range(1, n):
        to = lax.rem(me + i, n)
        push(sum_send.at[to], sum_recv.at[to], sum_ss, sum_rs, "seq", to, to).wait_recv()
        numerator = numerator + factors[i] * sum_recv[to].astype(f32)
    attention = numerator / denominator
    for h in range(own):
        att_all[mine, :, h * HD : (h + 1) * HD] = attention[
            h * requests : (h + 1) * requests
        ].astype(jnp.bfloat16)
    for i in range(1, nb):
        to = lax.rem(mine + i, nb)
        push(att_all.at[mine], att_all.at[mine], att_ss, att_rs, "batch", mine, to).start()
    for i in range(1, nb):
        to = lax.rem(mine + i, nb)
        push(att_all.at[mine], att_all.at[to], att_ss, att_rs, "batch", to, to).wait_recv()

    everyone = jnp.concatenate([att_all[b].astype(f32) for b in range(nb)], axis=0)
    projected = jnp.dot(everyone.astype(jnp.bfloat16), w_ref[...], preferred_element_type=f32)
    lines = out_ref.shape[0]
    for s in range(n):
        proj_send[s] = projected[s * lines : (s + 1) * lines].astype(proj_send.dtype)
    for i in range(1, n):
        to = lax.rem(me + i, n)
        push(proj_send.at[to], proj_recv.at[me], proj_ss, proj_rs, "seq", me, to).start()
    result = proj_send[me].astype(f32)
    for i in range(1, n):
        to = lax.rem(me + i, n)
        push(proj_send.at[to], proj_recv.at[to], proj_ss, proj_rs, "seq", to, to).wait_recv()
        result = result + proj_recv[to].astype(f32)
    out_ref[...] = result.astype(out_ref.dtype)

    for i in range(1, n):
        to = lax.rem(me + i, n)
        push(q_hbm, q_all.at[me], q_ss, q_rs, "seq", me, to).wait_send()
        push(stat_send.at[to], stat_recv.at[me], stat_ss, stat_rs, "seq", me, to).wait_send()
        push(sum_send.at[to], sum_recv.at[me], sum_ss, sum_rs, "seq", me, to).wait_send()
        push(proj_send.at[to], proj_recv.at[me], proj_ss, proj_rs, "seq", me, to).wait_send()
    for i in range(1, nb):
        to = lax.rem(mine + i, nb)
        push(att_all.at[mine], att_all.at[mine], att_ss, att_rs, "batch", mine, to).wait_send()


def on_device(n, nb, *args):
    queries, key_cache, value_cache, new_key, new_value, table, counts, offsets, w_out = args
    requests = queries.shape[0]
    own = HEADS // n
    lines = requests * nb // n
    columns = w_out.shape[1]
    bf16, f32 = jnp.bfloat16, jnp.float32
    hbm = pl.BlockSpec(memory_space=pl.ANY)
    smem = pl.BlockSpec(memory_space=pltpu.SMEM)
    dma = pltpu.SemaphoreType.DMA
    return pl.pallas_call(
        functools.partial(kernel, n, nb),
        out_shape=jax.ShapeDtypeStruct((lines, columns), bf16),
        in_specs=[hbm] * 5 + [smem] * 3 + [hbm],
        out_specs=pl.BlockSpec(memory_space=pltpu.VMEM),
        scratch_shapes=[
            pltpu.VMEM((n,) + queries.shape, bf16),
            pltpu.VMEM(key_cache.shape, bf16),
            pltpu.VMEM(value_cache.shape, bf16),
            pltpu.VMEM(new_key.shape, bf16),
            pltpu.VMEM(new_value.shape, bf16),
            pltpu.VMEM(w_out.shape, bf16),
            pltpu.VMEM((n, 2, HD), f32),
            pltpu.VMEM((n, 2, HD), f32),
            pltpu.VMEM((n, own * requests, HD), f32),
            pltpu.VMEM((n, own * requests, HD), f32),
            pltpu.VMEM((nb,) + queries.shape, bf16),
            pltpu.VMEM((n, lines, columns), f32),
            pltpu.VMEM((n, lines, columns), f32),
            dma((6,)),
            dma((n,)),
            dma((n,)),
            dma((n,)),
            dma((n,)),
            dma((n,)),
            dma((n,)),
            dma((nb,)),
            dma((nb,)),
            dma((n,)),
            dma((n,)),
        ],
        compiler_params=pltpu.CompilerParams(collective_id=0, has_side_effects=True),
    )(*args)


def solution(mesh):
    placed = (
        P("batch", "seq"),
        P("batch", "seq", None),
        P("batch", "seq", None),
        P("batch", None),
        P("batch", None),
        P("batch", "seq"),
        P("batch", "seq"),
        P("batch"),
        P("seq", "batch"),
    )
    return jax.shard_map(
        functools.partial(on_device, mesh.shape["seq"], mesh.shape["batch"]),
        mesh=mesh,
        in_specs=placed,
        out_specs=P("seq", "batch"),
        check_vma=False,
    )
```

time: 98.3 us -> 27.1 us (0.28)
  blocking collectives: 73.8 us -> 0 us
  Pallas kernels: 0 us -> 23 us
  local copies, waits for them, and re-layouts: 11.6 us -> 3.92 us
  other arithmetic: 6.21 us -> 0 us
  matrix products: 5.44 us -> 0 us
    all_gather x5 -> x0, blocking collectives: 50.7 us -> none  [the longest x3 26.6 us: joined(): everything = jax.tree.map(lambda part: lax.all_gather(part, axis), x)]
    unnamed x1 -> x0, blocking collectives: 23.1 us -> none
    pallas_call x0 -> x1, Pallas kernels: none -> 23 us  [on_device(): pl.pallas_call(functools.partial(kernel, n, nb), out_shape=jax.ShapeDtype...]
    gather x2 -> x0, local copies, waits for them, and re-layouts: 5.6 us -> none  [the longest x1 3.58 us: on_device(): jnp.take(value_cache, page_table, axis=0)]
    dot_general x4 -> x0, matrix products: 5.44 us -> none  [the longest x1 3.01 us: on_device(): jnp.einsum('bkgd,btkd->bkgt', query_lattice, key_rows, preferred_element_...]
    select_n x1 -> x0, other arithmetic: 3.96 us -> none  [on_device(): jnp.take(value_cache, page_table, axis=0)]
    unnamed x24 -> x3, local copies, waits for them, and re-layouts: 4.04 us -> 3.92 us
where the time goes in v1:
time: 27.1 us; the launch traced here: 26.9 us
  Pallas kernels  23 us (85%)
  local copies, waits for them, and re-layouts  3.92 us (14%)
    pallas_call x1, Pallas kernels, on_device(): pl.pallas_call(functools.partial(kernel, n, nb), out_shape=jax.ShapeDtype...  23 us
    unnamed x3, local copies, waits for them, and re-layouts  3.92 us

profile of v1, /device:TPU:0, one launch (start us, length us, event | category | flops | bytes accessed | tf_op | source)
XLA Modules:
  0.0 26.9 jit_solution(2374789203252456869)
XLA Ops:
  0.0 1.3 %copy.10.table = s32[4,1]{1,0:T(4,128)} copy(s32[4,1]{0,1:T(1,128)} %param.14) | data formatting | bytes 32 | tf_op args[5]
  1.3 1.3 %copy.11.counts = s32[4,1]{1,0:T(4,128)} copy(s32[4,1]{0,1:T(1,128)} %param.15) | data formatting | bytes 32 | tf_op args[6]
  2.6 23.0 %shard_map.91 = bf16[2,1152]{1,0:T(2,128)(2,1)} custom-call(bf16[4,512]{1,0:T(4,128)(2,1)} %q_hbm.1, bf16[4,128,2048]{2,1,0:T(8,128)(2,1)} %k_hbm.1, bf16[4,128,2048]{2,1,0:T(8,128)(2,1)} %v_hbm.1, bf16[4,2048]{1,0:T(4,128)(2,1)} %nk_hbm.1, bf16[4,2048]{1,0:T(4,128)(2,1)} %nv_hbm.1, s32[4,1]{1,0:T(4,128)} %copy.10.table, s32[4,1]{1,0:T(4,128)} %copy.11.counts, ...), custom_call_target="tpu_custom_call" | custom-call | tf_op jit(solution)/shard_map/pallas_call | solution.py:276
  25.6 1.3 %copy.13 = bf16[2,1152]{1,0:T(2,128)(2,1)} copy(bf16[2,1152]{1,0:T(2,128)(2,1)} %shard_map.91) | data formatting | bytes 9216

commit v2 on v1

--- a/solution.py
+++ b/solution.py
@@ -58,7 +58,7 @@
     mine = lax.axis_index("batch")
     requests = q_hbm.shape[0]
     slots, page_len, _ = k_hbm.shape
-    pages = table.shape[1]
+    pages = table.shape[0]
     tokens = slots * page_len
     groups = HEADS // KVH
     own = HEADS // n
@@ -115,8 +115,8 @@
         where_at = jnp.zeros((rows, tokens), jnp.int32)
         count = jnp.zeros((rows, tokens), jnp.int32)
         for r in range(requests):
-            where_at = jnp.where(row_request == r, table[r, p], where_at)
-            count = jnp.where(row_request == r, counts[r, p], count)
+            where_at = jnp.where(row_request == r, table[p, r], where_at)
+            count = jnp.where(row_request == r, counts[p, r], count)
         start = (me * pages + p) * page_len
         live = live | ((where_at == slot) & (token < count) & (start + token >= first))
 
@@ -275,7 +275,7 @@
     dma = pltpu.SemaphoreType.DMA
     return pl.pallas_call(
         functools.partial(kernel, n, nb),
-        out_shape=jax.ShapeDtypeStruct((lines, columns), bf16),
+        out_shape=pltpu.VMEM((lines, columns), bf16),
         in_specs=[hbm] * 5 + [smem] * 3 + [hbm],
         out_specs=pl.BlockSpec(memory_space=pltpu.VMEM),
         scratch_shapes=[
@@ -305,7 +305,7 @@
             dma((n,)),
         ],
         compiler_params=pltpu.CompilerParams(collective_id=0, has_side_effects=True),
-    )(*args)
+    )(*args[:5], table.T, counts.T, offsets, w_out)
 
 
 def solution(mesh):

time: 27.1 us -> 23.1 us (0.85)
  local copies, waits for them, and re-layouts: 3.92 us -> 0.6 us
  Pallas kernels: 23 us -> 22.3 us
    unnamed x3 -> x1, local copies, waits for them, and re-layouts: 3.92 us -> 0.6 us
    pallas_call x1, Pallas kernels: 23 us -> 22.3 us  [on_device(): pl.pallas_call(functools.partial(kernel, n, nb), out_shape=pltpu.VMEM((li...]
where the time goes in v2:
time: 23.1 us; the launch traced here: 22.9 us
  Pallas kernels  22.3 us (97%)
  local copies, waits for them, and re-layouts  0.6 us (3%)
    pallas_call x1, Pallas kernels, on_device(): pl.pallas_call(functools.partial(kernel, n, nb), out_shape=pltpu.VMEM((li...  22.3 us
    unnamed x1, local copies, waits for them, and re-layouts  0.6 us

profile of v2, /device:TPU:0, one launch (start us, length us, event | category | flops | bytes accessed | tf_op | source)
XLA Modules:
  0.0 22.9 jit_solution(10794150201598198615)
XLA Ops:
  0.0 22.3 %shard_map.91 = bf16[2,1152]{1,0:T(2,128)(2,1)S(1)} custom-call(bf16[4,512]{1,0:T(4,128)(2,1)} %q_hbm.1, bf16[4,128,2048]{2,1,0:T(8,128)(2,1)} %k_hbm.1, bf16[4,128,2048]{2,1,0:T(8,128)(2,1)} %v_hbm.1, bf16[4,2048]{1,0:T(4,128)(2,1)} %nk_hbm.1, bf16[4,2048]{1,0:T(4,128)(2,1)} %nv_hbm.1, s32[1,4]{1,0:T(1,128)} %bitcast.2, s32[1,4]{1,0:T(1,128)} %bitcast.3, ...), custom_call_target="tpu_custom_call" | custom-call | tf_op jit(solution)/shard_map/pallas_call | solution.py:276
  22.3 0.6 %copy.11 = bf16[2,1152]{1,0:T(2,128)(2,1)} copy(bf16[2,1152]{1,0:T(2,128)(2,1)S(1)} %shard_map.91) | data formatting | bytes 9216

commit v3 on v2

v3 whole, which is shorter than its diff:
```python
import functools

import jax
import jax.numpy as jnp
from jax import lax
from jax.experimental import pallas as pl
from jax.experimental.pallas import tpu as pltpu
from jax.sharding import PartitionSpec as P

HEADS = 32
KVH = 16
HD = 128
QSCALAR = 144
CHUNK = 2

floor_score = -1e30


def kernel(
    n,
    nb,
    q_hbm,
    k_hbm,
    v_hbm,
    nk_hbm,
    nv_hbm,
    table_hbm,
    counts_hbm,
    offsets_hbm,
    w_hbm,
    out_ref,
    q_all,
    k_ref,
    v_ref,
    nk_ref,
    nv_ref,
    w_ref,
    table,
    counts,
    offsets,
    stat_send,
    stat_recv,
    sum_send,
    sum_recv,
    att_all,
    proj_send,
    proj_recv,
    load_sem,
    q_ss,
    q_rs,
    stat_ss,
    stat_rs,
    sum_ss,
    sum_rs,
    att_ss,
    att_rs,
    proj_ss,
    proj_rs,
):
    me = lax.axis_index("seq")
    mine = lax.axis_index("batch")
    requests = q_hbm.shape[0]
    slots, page_len, _ = k_hbm.shape
    pages = table_hbm.shape[0]
    tokens = slots * page_len
    groups = HEADS // KVH
    own = HEADS // n
    width = CHUNK * HD
    chunk_heads = CHUNK * groups
    rows = chunk_heads * requests
    n_chunks = KVH // CHUNK
    scale = QSCALAR ** (-0.5)
    f32 = jnp.float32

    loads = [
        pltpu.make_async_copy(src, dst, load_sem.at[i])
        for i, (src, dst) in enumerate(
            (
                (q_hbm, q_all.at[me]),
                (k_hbm, k_ref),
                (v_hbm, v_ref),
                (table_hbm, table),
                (counts_hbm, counts),
                (offsets_hbm, offsets),
                (nk_hbm, nk_ref),
                (nv_hbm, nv_ref),
                (w_hbm, w_ref),
            )
        )
    ]
    for load in loads:
        load.start()

    def partner(place, m):
        to, bit = place, 1
        while bit <= m:
            if m & bit:
                to = to + bit * (1 - 2 * ((place // bit) % 2))
            bit *= 2
        return to

    far_first = [partner(me, m) for m in range(n - 1, 0, -1)]
    near_first = far_first[::-1]
    far_batch = [partner(mine, m) for m in range(nb - 1, 0, -1)]

    barrier = pltpu.get_barrier_semaphore()
    for to in far_batch:
        pl.semaphore_signal(barrier, inc=1, device_id={"batch": to})
    for to in far_first:
        pl.semaphore_signal(barrier, inc=1, device_id={"seq": to})
    loads[0].wait()
    pl.semaphore_wait(barrier, n - 1 + nb - 1)

    def push(src, dst, ss, rs, axis, place, to):
        return pltpu.make_async_remote_copy(
            src_ref=src,
            dst_ref=dst,
            send_sem=ss.at[to],
            recv_sem=rs.at[place],
            device_id={axis: to},
        )

    def push_q(place, to):
        return push(q_all.at[me], q_all.at[place], q_ss, q_rs, "seq", place, to)

    def push_stat(place, to):
        return push(stat_send.at[to], stat_recv.at[place], stat_ss, stat_rs, "seq", place, to)

    def push_sum(place, to):
        return push(sum_send.at[to], sum_recv.at[place], sum_ss, sum_rs, "seq", place, to)

    def push_att(place, to):
        return push(att_all.at[mine], att_all.at[place], att_ss, att_rs, "batch", place, to)

    def push_proj(place, to):
        return push(proj_send.at[to], proj_recv.at[place], proj_ss, proj_rs, "seq", place, to)

    for to in far_first:
        push_q(me, to).start()
    for load in loads[1:6]:
        load.wait()

    row_request = lax.broadcasted_iota(jnp.int32, (rows, tokens), 0) % requests
    column = lax.broadcasted_iota(jnp.int32, (rows, tokens), 1)
    slot, token = column // page_len, column % page_len
    live = jnp.zeros((rows, tokens), jnp.bool_)
    first = jnp.zeros((rows, tokens), jnp.int32)
    for r in range(requests):
        first = jnp.where(row_request == r, offsets[0, r], first)
    for p in range(pages):
        where_at = jnp.zeros((rows, tokens), jnp.int32)
        count = jnp.zeros((rows, tokens), jnp.int32)
        for r in range(requests):
            where_at = jnp.where(row_request == r, table[p, r], where_at)
            count = jnp.where(row_request == r, counts[p, r], count)
        start = (me * pages + p) * page_len
        live = live | ((where_at == slot) & (token < count) & (start + token >= first))

    row = lax.broadcasted_iota(jnp.int32, (rows, HD), 0)
    lane = lax.broadcasted_iota(jnp.int32, (rows, HD), 1)

    def head_rows(ref, lead, head):
        at = pl.ds(pl.multiple_of(head * HD, HD), HD)
        return (ref[lead, :, at] if lead is not None else ref[:, at]).astype(f32)

    base = (me * own) // chunk_heads
    span = min(own, chunk_heads)
    per_chunk = chunk_heads // span
    half = groups * requests

    def unless_mine(step, to, run):
        if step:
            run()
        elif per_chunk > 1:
            pl.when(to != me)(run)

    def scores_of(c):
        at = pl.ds(pl.multiple_of(c * width, width), width)
        head0 = c * chunk_heads
        parts = []
        for h in range(chunk_heads):
            parts.append(head_rows(q_all, (head0 + h) // own, (head0 + h) % own))
        q = jnp.concatenate(parts, axis=0)
        wide = jnp.concatenate(
            [jnp.where(row // half == k, q, 0.0).astype(jnp.bfloat16) for k in range(CHUNK)],
            axis=1,
        )
        keys = k_ref[:, :, at].reshape(tokens, width)
        return lax.dot_general(wide, keys, (((1,), (1,)), ((), ())), preferred_element_type=f32)

    def softmax_of(scores):
        scores = scores * scale
        peak = jnp.max(jnp.where(live, scores, floor_score), axis=1, keepdims=True)
        weights = jnp.where(live, jnp.exp(scores - peak), 0.0)
        return peak, jnp.sum(weights, axis=1, keepdims=True), weights.astype(jnp.bfloat16)

    def sums_of(c, weights):
        at = pl.ds(pl.multiple_of(c * width, width), width)
        values = v_ref[:, :, at].reshape(tokens, width)
        full = jnp.dot(weights, values, preferred_element_type=f32)
        return jnp.concatenate(
            [full[k * half : (k + 1) * half, k * HD : (k + 1) * HD] for k in range(CHUNK)], axis=0
        )

    near = [m for m in range(2, n_chunks) if m < n_chunks - n_chunks // 4]
    far = [m for m in range(2, n_chunks) if m not in near]
    for steps in ([0], [1], near, far):
        chunks = [partner(base, m) for m in steps]
        for m, c in zip(steps, chunks):
            for part in range(per_chunk):
                src = c * per_chunk + part
                unless_mine(m, src, lambda src=src: push_q(src, src).wait_recv())
        scores = [scores_of(c) for c in chunks]
        soft = [softmax_of(x) for x in scores]
        sums = [sums_of(c, x[2]) for c, x in zip(chunks, soft)]
        height = span * requests
        for m, c, (peak, total, _), done in zip(steps, chunks, soft, sums):
            for part in range(per_chunk):
                to = c * per_chunk + part
                low = part * height
                hit = (row - low == lane) & (row >= low) & (row < low + height)
                stat_send[to] = jnp.concatenate(
                    [
                        jnp.sum(jnp.where(hit, peak, 0.0), axis=0, keepdims=True),
                        jnp.sum(jnp.where(hit, total, 0.0), axis=0, keepdims=True),
                    ],
                    axis=0,
                )
                sum_send[to] = done[low : low + height].astype(sum_send.dtype)
        for m, c in zip(steps, chunks):
            for part in range(per_chunk):
                to = c * per_chunk + part

                def send(to=to):
                    push_sum(me, to).start()
                    push_stat(me, to).start()

                unless_mine(m, to, send)

    own_rows = own * requests
    for load in loads[6:]:
        load.wait()
    kv = [(me * own + h) // groups for h in range(own)]
    own_q = jnp.concatenate([head_rows(q_all, me, h) for h in range(own)], axis=0)
    own_key = jnp.concatenate([head_rows(nk_ref, None, k) for k in kv], axis=0)
    own_value = jnp.concatenate([head_rows(nv_ref, None, k) for k in kv], axis=0)
    new_score = jnp.sum(own_q * own_key, axis=1, keepdims=True) * scale

    o_row = lax.broadcasted_iota(jnp.int32, (own_rows, HD), 0)
    o_lane = lax.broadcasted_iota(jnp.int32, (own_rows, HD), 1)
    diagonal = o_row == o_lane

    def to_column(line):
        return jnp.sum(jnp.where(diagonal, line, 0.0), axis=1, keepdims=True)

    for to in near_first:
        push_stat(to, to).wait_recv()
    stats = [stat_send[me]] + [stat_recv[to] for to in near_first]
    peaks = [to_column(s[0:1]) for s in stats]
    totals = [to_column(s[1:2]) for s in stats]
    top = new_score
    for peak in peaks:
        top = jnp.maximum(top, peak)
    own_weight = jnp.exp(new_score - top)
    factors = [jnp.exp(peak - top) for peak in peaks]
    denominator = own_weight
    for total, factor in zip(totals, factors):
        denominator = denominator + total * factor
    numerator = own_weight * own_value + factors[0] * sum_send[me].astype(f32)
    for to, factor in zip(near_first, factors[1:]):
        push_sum(to, to).wait_recv()
        numerator = numerator + factor * sum_recv[to].astype(f32)
    attention = numerator / denominator
    for h in range(own):
        att_all[mine, :, h * HD : (h + 1) * HD] = attention[
            h * requests : (h + 1) * requests
        ].astype(jnp.bfloat16)
    for to in far_batch:
        push_att(mine, to).start()
    for to in far_batch:
        push_att(to, to).wait_recv()

    everyone = jnp.concatenate([att_all[b].astype(f32) for b in range(nb)], axis=0)
    projected = jnp.dot(everyone.astype(jnp.bfloat16), w_ref[...], preferred_element_type=f32)
    lines = out_ref.shape[0]
    for s in range(n):
        proj_send[s] = projected[s * lines : (s + 1) * lines].astype(proj_send.dtype)
    for to in far_first:
        push_proj(me, to).start()
    result = proj_send[me].astype(f32)
    for to in near_first:
        push_proj(to, to).wait_recv()
        result = result + proj_recv[to].astype(f32)
    out_ref[...] = result.astype(out_ref.dtype)

    for to in far_first:
        for sent in (push_q, push_stat, push_sum, push_proj):
            sent(me, to).wait_send()
    for to in far_batch:
        push_att(mine, to).wait_send()


def on_device(n, nb, *args):
    queries, key_cache, value_cache, new_key, new_value, table, counts, offsets, w_out = args
    requests = queries.shape[0]
    own = HEADS // n
    lines = requests * nb // n
    columns = w_out.shape[1]
    bf16, f32 = jnp.bfloat16, jnp.float32
    hbm = pl.BlockSpec(memory_space=pl.ANY)
    dma = pltpu.SemaphoreType.DMA
    return pl.pallas_call(
        functools.partial(kernel, n, nb),
        out_shape=pltpu.VMEM((lines, columns), bf16),
        in_specs=[hbm] * 9,
        out_specs=pl.BlockSpec(memory_space=pltpu.VMEM),
        scratch_shapes=[
            pltpu.VMEM((n,) + queries.shape, bf16),
            pltpu.VMEM(key_cache.shape, bf16),
            pltpu.VMEM(value_cache.shape, bf16),
            pltpu.VMEM(new_key.shape, bf16),
            pltpu.VMEM(new_value.shape, bf16),
            pltpu.VMEM(w_out.shape, bf16),
            pltpu.SMEM(table.T.shape, jnp.int32),
            pltpu.SMEM(counts.T.shape, jnp.int32),
            pltpu.SMEM((1,) + offsets.shape, jnp.int32),
            pltpu.VMEM((n, 2, HD), f32),
            pltpu.VMEM((n, 2, HD), f32),
            pltpu.VMEM((n, own * requests, HD), bf16),
            pltpu.VMEM((n, own * requests, HD), bf16),
            pltpu.VMEM((nb,) + queries.shape, bf16),
            pltpu.VMEM((n, lines, columns), bf16),
            pltpu.VMEM((n, lines, columns), bf16),
            dma((9,)),
            dma((n,)),
            dma((n,)),
            dma((n,)),
            dma((n,)),
            dma((n,)),
            dma((n,)),
            dma((nb,)),
            dma((nb,)),
            dma((n,)),
            dma((n,)),
        ],
        compiler_params=pltpu.CompilerParams(collective_id=0, has_side_effects=True),
    )(*args[:5], table.T, counts.T, offsets[None], w_out)


def solution(mesh):
    placed = (
        P("batch", "seq"),
        P("batch", "seq", None),
        P("batch", "seq", None),
        P("batch", None),
        P("batch", None),
        P("batch", "seq"),
        P("batch", "seq"),
        P("batch"),
        P("seq", "batch"),
    )
    return jax.shard_map(
        functools.partial(on_device, mesh.shape["seq"], mesh.shape["batch"]),
        mesh=mesh,
        in_specs=placed,
        out_specs=P("seq", "batch"),
        check_vma=False,
    )
```

time: 23.1 us -> 20.8 us (0.900)
  Pallas kernels: 22.3 us -> 20.1 us
    pallas_call x1, Pallas kernels: 22.3 us -> 20.1 us  [on_device(): pl.pallas_call(functools.partial(kernel, n, nb), out_shape=pltpu.VMEM((li...]
where the time goes in v3:
time: 20.8 us; the launch traced here: 20.7 us
  Pallas kernels  20.1 us (97%)
  local copies, waits for them, and re-layouts  0.6 us (3%)
    pallas_call x1, Pallas kernels, on_device(): pl.pallas_call(functools.partial(kernel, n, nb), out_shape=pltpu.VMEM((li...  20.1 us
    unnamed x1, local copies, waits for them, and re-layouts  0.6 us

profile of v3, /device:TPU:0, one launch (start us, length us, event | category | flops | bytes accessed | tf_op | source)
XLA Modules:
  0.0 20.7 jit_solution(6288863012996462910)
XLA Ops:
  0.0 20.1 %shard_map.91 = bf16[2,1152]{1,0:T(2,128)(2,1)S(1)} custom-call(bf16[4,512]{1,0:T(4,128)(2,1)} %q_hbm.1, bf16[4,128,2048]{2,1,0:T(8,128)(2,1)} %k_hbm.1, bf16[4,128,2048]{2,1,0:T(8,128)(2,1)} %v_hbm.1, bf16[4,2048]{1,0:T(4,128)(2,1)} %nk_hbm.1, bf16[4,2048]{1,0:T(4,128)(2,1)} %nv_hbm.1, s32[1,4]{1,0:T(1,128)} %bitcast.3, s32[1,4]{1,0:T(1,128)} %bitcast.4, ...), custom_call_target="tpu_custom_call" | custom-call | tf_op jit(solution)/shard_map/pallas_call | solution.py:312
  20.1 0.6 %copy.11 = bf16[2,1152]{1,0:T(2,128)(2,1)} copy(bf16[2,1152]{1,0:T(2,128)(2,1)S(1)} %shard_map.91) | data formatting | bytes 9216

commit v4 on v3

--- a/solution.py
+++ b/solution.py
@@ -30,13 +30,10 @@
     w_hbm,
     out_ref,
     q_all,
-    k_ref,
-    v_ref,
-    nk_ref,
-    nv_ref,
+    pools,
+    fresh,
     w_ref,
-    table,
-    counts,
+    small,
     offsets,
     stat_send,
     stat_recv,
@@ -46,16 +43,9 @@
     proj_send,
     proj_recv,
     load_sem,
-    q_ss,
+    send_sem,
+    recv_sem,
     q_rs,
-    stat_ss,
-    stat_rs,
-    sum_ss,
-    sum_rs,
-    att_ss,
-    att_rs,
-    proj_ss,
-    proj_rs,
 ):
     me = lax.axis_index("seq")
     mine = lax.axis_index("batch")
@@ -72,24 +62,27 @@
     scale = QSCALAR ** (-0.5)
     f32 = jnp.float32
 
-    loads = [
-        pltpu.make_async_copy(src, dst, load_sem.at[i])
-        for i, (src, dst) in enumerate(
-            (
-                (q_hbm, q_all.at[me]),
-                (k_hbm, k_ref),
-                (v_hbm, v_ref),
-                (table_hbm, table),
-                (counts_hbm, counts),
-                (offsets_hbm, offsets),
-                (nk_hbm, nk_ref),
-                (nv_hbm, nv_ref),
-                (w_hbm, w_ref),
-            )
-        )
-    ]
-    for load in loads:
-        load.start()
+    def load(sources, held, sem):
+        for i, src in enumerate(sources):
+            pltpu.make_async_copy(src, held.at[i], load_sem.at[sem]).start()
+
+        def wait():
+            pltpu.make_async_copy(held, held, load_sem.at[sem]).wait()
+
+        return wait
+
+    q_load = pltpu.make_async_copy(q_hbm, q_all.at[me], load_sem.at[0])
+    q_load.start()
+    wait_pages = load((k_hbm, v_hbm), pools, 1)
+    wait_small = load((table_hbm, counts_hbm), small, 2)
+    offsets_load = pltpu.make_async_copy(offsets_hbm, offsets, load_sem.at[3])
+    offsets_load.start()
+    wait_new = load((nk_hbm, nv_hbm), fresh, 4)
+    w_load = pltpu.make_async_copy(w_hbm, w_ref, load_sem.at[5])
+    w_load.start()
+    k_ref, v_ref = pools.at[0], pools.at[1]
+    nk_ref, nv_ref = fresh.at[0], fresh.at[1]
+    table, counts = small.at[0], small.at[1]
 
     def partner(place, m):
         to, bit = place, 1
@@ -108,37 +101,43 @@
         pl.semaphore_signal(barrier, inc=1, device_id={"batch": to})
     for to in far_first:
         pl.semaphore_signal(barrier, inc=1, device_id={"seq": to})
-    loads[0].wait()
+    q_load.wait()
     pl.semaphore_wait(barrier, n - 1 + nb - 1)
 
-    def push(src, dst, ss, rs, axis, place, to):
+    def push(src, dst, ss, rs, axis, to):
         return pltpu.make_async_remote_copy(
-            src_ref=src,
-            dst_ref=dst,
-            send_sem=ss.at[to],
-            recv_sem=rs.at[place],
-            device_id={axis: to},
+            src_ref=src, dst_ref=dst, send_sem=ss, recv_sem=rs, device_id={axis: to}
         )
 
-    def push_q(place, to):
-        return push(q_all.at[me], q_all.at[place], q_ss, q_rs, "seq", place, to)
-
-    def push_stat(place, to):
-        return push(stat_send.at[to], stat_recv.at[place], stat_ss, stat_rs, "seq", place, to)
-
-    def push_sum(place, to):
-        return push(sum_send.at[to], sum_recv.at[place], sum_ss, sum_rs, "seq", place, to)
-
-    def push_att(place, to):
-        return push(att_all.at[mine], att_all.at[place], att_ss, att_rs, "batch", place, to)
-
-    def push_proj(place, to):
-        return push(proj_send.at[to], proj_recv.at[place], proj_ss, proj_rs, "seq", place, to)
-
-    for to in far_first:
-        push_q(me, to).start()
-    for load in loads[1:6]:
-        load.wait()
+    def wait_bytes(buffer, parts, sem):
+        if parts:
+            some = buffer.at[pl.ds(0, parts)]
+            pltpu.make_async_copy(some, some, sem).wait()
+
+    def push_q(to, step):
+        push(q_all.at[me], q_all.at[me], send_sem.at[0], q_rs.at[min(step, 2)], "seq", to).start()
+
+    def push_stat(to):
+        push(stat_send.at[to], stat_recv.at[me], send_sem.at[1], recv_sem.at[0], "seq", to).start()
+
+    def push_sum(to):
+        push(sum_send.at[to], sum_recv.at[me], send_sem.at[2], recv_sem.at[1], "seq", to).start()
+
+    def push_att(to):
+        mine_at = att_all.at[mine]
+        push(mine_at, mine_at, send_sem.at[3], recv_sem.at[2], "batch", to).start()
+
+    def push_proj(to):
+        push(proj_send.at[to], proj_recv.at[me], send_sem.at[4], recv_sem.at[3], "seq", to).start()
+
+    base = (me * own) // chunk_heads
+    span = min(own, chunk_heads)
+    per_chunk = chunk_heads // span
+    half = groups * requests
+    for m in range(n - 1, 0, -1):
+        push_q(partner(me, m), m // per_chunk)
+    wait_small()
+    offsets_load.wait()
 
     row_request = lax.broadcasted_iota(jnp.int32, (rows, tokens), 0) % requests
     column = lax.broadcasted_iota(jnp.int32, (rows, tokens), 1)
@@ -163,10 +162,15 @@
         at = pl.ds(pl.multiple_of(head * HD, HD), HD)
         return (ref[lead, :, at] if lead is not None else ref[:, at]).astype(f32)
 
-    base = (me * own) // chunk_heads
-    span = min(own, chunk_heads)
-    per_chunk = chunk_heads // span
-    half = groups * requests
+    own_rows = own * requests
+    wait_new()
+    kv = [(me * own + h) // groups for h in range(own)]
+    own_q = jnp.concatenate([head_rows(q_all, me, h) for h in range(own)], axis=0)
+    own_key = jnp.concatenate([head_rows(nk_ref, None, k) for k in kv], axis=0)
+    own_value = jnp.concatenate([head_rows(nv_ref, None, k) for k in kv], axis=0)
+    new_score = jnp.sum(own_q * own_key, axis=1, keepdims=True) * scale
+
+    wait_pages()
 
     def unless_mine(step, to, run):
         if step:
@@ -202,14 +206,9 @@
             [full[k * half : (k + 1) * half, k * HD : (k + 1) * HD] for k in range(CHUNK)], axis=0
         )
 
-    near = [m for m in range(2, n_chunks) if m < n_chunks - n_chunks // 4]
-    far = [m for m in range(2, n_chunks) if m not in near]
-    for steps in ([0], [1], near, far):
+    for steps in ([0], [1], list(range(n_chunks - 1, 1, -1))):
         chunks = [partner(base, m) for m in steps]
-        for m, c in zip(steps, chunks):
-            for part in range(per_chunk):
-                src = c * per_chunk + part
-                unless_mine(m, src, lambda src=src: push_q(src, src).wait_recv())
+        wait_bytes(q_all, per_chunk * len(steps) - (0 in steps), q_rs.at[min(steps[-1], 2)])
         scores = [scores_of(c) for c in chunks]
         soft = [softmax_of(x) for x in scores]
         sums = [sums_of(c, x[2]) for c, x in zip(chunks, soft)]
@@ -232,19 +231,10 @@
                 to = c * per_chunk + part
 
                 def send(to=to):
-                    push_sum(me, to).start()
-                    push_stat(me, to).start()
+                    push_sum(to)
+                    push_stat(to)
 
                 unless_mine(m, to, send)
-
-    own_rows = own * requests
-    for load in loads[6:]:
-        load.wait()
-    kv = [(me * own + h) // groups for h in range(own)]
-    own_q = jnp.concatenate([head_rows(q_all, me, h) for h in range(own)], axis=0)
-    own_key = jnp.concatenate([head_rows(nk_ref, None, k) for k in kv], axis=0)
-    own_value = jnp.concatenate([head_rows(nv_ref, None, k) for k in kv], axis=0)
-    new_score = jnp.sum(own_q * own_key, axis=1, keepdims=True) * scale
 
     o_row = lax.broadcasted_iota(jnp.int32, (own_rows, HD), 0)
     o_lane = lax.broadcasted_iota(jnp.int32, (own_rows, HD), 1)
@@ -253,8 +243,7 @@
     def to_column(line):
         return jnp.sum(jnp.where(diagonal, line, 0.0), axis=1, keepdims=True)
 
-    for to in near_first:
-        push_stat(to, to).wait_recv()
+    wait_bytes(stat_recv, n - 1, recv_sem.at[0])
     stats = [stat_send[me]] + [stat_recv[to] for to in near_first]
     peaks = [to_column(s[0:1]) for s in stats]
     totals = [to_column(s[1:2]) for s in stats]
@@ -267,8 +256,8 @@
     for total, factor in zip(totals, factors):
         denominator = denominator + total * factor
     numerator = own_weight * own_value + factors[0] * sum_send[me].astype(f32)
+    wait_bytes(sum_recv, n - 1, recv_sem.at[1])
     for to, factor in zip(near_first, factors[1:]):
-        push_sum(to, to).wait_recv()
         numerator = numerator + factor * sum_recv[to].astype(f32)
     attention = numerator / denominator
     for h in range(own):
@@ -276,9 +265,9 @@
             h * requests : (h + 1) * requests
         ].astype(jnp.bfloat16)
     for to in far_batch:
-        push_att(mine, to).start()
-    for to in far_batch:
-        push_att(to, to).wait_recv()
+        push_att(to)
+    w_load.wait()
+    wait_bytes(att_all, nb - 1, recv_sem.at[2])
 
     everyone = jnp.concatenate([att_all[b].astype(f32) for b in range(nb)], axis=0)
     projected = jnp.dot(everyone.astype(jnp.bfloat16), w_ref[...], preferred_element_type=f32)
@@ -286,18 +275,18 @@
     for s in range(n):
         proj_send[s] = projected[s * lines : (s + 1) * lines].astype(proj_send.dtype)
     for to in far_first:
-        push_proj(me, to).start()
+        push_proj(to)
     result = proj_send[me].astype(f32)
+    wait_bytes(proj_recv, n - 1, recv_sem.at[3])
     for to in near_first:
-        push_proj(to, to).wait_recv()
         result = result + proj_recv[to].astype(f32)
     out_ref[...] = result.astype(out_ref.dtype)
 
-    for to in far_first:
-        for sent in (push_q, push_stat, push_sum, push_proj):
-            sent(me, to).wait_send()
-    for to in far_batch:
-        push_att(mine, to).wait_send()
+    wait_bytes(q_all, n - 1, send_sem.at[0])
+    wait_bytes(stat_send, n - 1, send_sem.at[1])
+    wait_bytes(sum_send, n - 1, send_sem.at[2])
+    wait_bytes(att_all, nb - 1, send_sem.at[3])
+    wait_bytes(proj_send, n - 1, send_sem.at[4])
 
 
 def on_device(n, nb, *args):
@@ -316,32 +305,22 @@
         out_specs=pl.BlockSpec(memory_space=pltpu.VMEM),
         scratch_shapes=[
             pltpu.VMEM((n,) + queries.shape, bf16),
-            pltpu.VMEM(key_cache.shape, bf16),
-            pltpu.VMEM(value_cache.shape, bf16),
-            pltpu.VMEM(new_key.shape, bf16),
-            pltpu.VMEM(new_value.shape, bf16),
+            pltpu.VMEM((2,) + key_cache.shape, bf16),
+            pltpu.VMEM((2,) + new_key.shape, bf16),
             pltpu.VMEM(w_out.shape, bf16),
-            pltpu.SMEM(table.T.shape, jnp.int32),
-            pltpu.SMEM(counts.T.shape, jnp.int32),
+            pltpu.SMEM((2,) + table.T.shape, jnp.int32),
             pltpu.SMEM((1,) + offsets.shape, jnp.int32),
             pltpu.VMEM((n, 2, HD), f32),
             pltpu.VMEM((n, 2, HD), f32),
             pltpu.VMEM((n, own * requests, HD), bf16),
             pltpu.VMEM((n, own * requests, HD), bf16),
             pltpu.VMEM((nb,) + queries.shape, bf16),
-            pltpu.VMEM((n, lines, columns), bf16),
-            pltpu.VMEM((n, lines, columns), bf16),
-            dma((9,)),
-            dma((n,)),
-            dma((n,)),
-            dma((n,)),
-            dma((n,)),
-            dma((n,)),
-            dma((n,)),
-            dma((nb,)),
-            dma((nb,)),
-            dma((n,)),
-            dma((n,)),
+            pltpu.VMEM((n, lines, columns), f32),
+            pltpu.VMEM((n, lines, columns), f32),
+            dma((6,)),
+            dma((5,)),
+            dma((4,)),
+            dma((3,)),
         ],
         compiler_params=pltpu.CompilerParams(collective_id=0, has_side_effects=True),
     )(*args[:5], table.T, counts.T, offsets[None], w_out)

time: 20.8 us -> 20.1 us (0.966)
  Pallas kernels: 20.1 us -> 19.3 us
    pallas_call x1, Pallas kernels: 20.1 us -> 19.3 us  [on_device(): pl.pallas_call(functools.partial(kernel, n, nb), out_shape=pltpu.VMEM((li...]
where the time goes in v4:
time: 20.1 us; the launch traced here: 19.9 us
  Pallas kernels  19.3 us (96%)
  local copies, waits for them, and re-layouts  0.6 us (3%)
    pallas_call x1, Pallas kernels, on_device(): pl.pallas_call(functools.partial(kernel, n, nb), out_shape=pltpu.VMEM((li...  19.3 us
    unnamed x1, local copies, waits for them, and re-layouts  0.6 us

profile of v4, /device:TPU:0, one launch (start us, length us, event | category | flops | bytes accessed | tf_op | source)
XLA Modules:
  0.0 19.9 jit_solution(13611433904138230019)
XLA Ops:
  0.0 19.3 %shard_map.91 = bf16[2,1152]{1,0:T(2,128)(2,1)S(1)} custom-call(bf16[4,512]{1,0:T(4,128)(2,1)} %q_hbm.1, bf16[4,128,2048]{2,1,0:T(8,128)(2,1)} %k_hbm.1, bf16[4,128,2048]{2,1,0:T(8,128)(2,1)} %v_hbm.1, bf16[4,2048]{1,0:T(4,128)(2,1)} %nk_hbm.1, bf16[4,2048]{1,0:T(4,128)(2,1)} %nv_hbm.1, s32[1,4]{1,0:T(1,128)} %bitcast.3, s32[1,4]{1,0:T(1,128)} %bitcast.4, ...), custom_call_target="tpu_custom_call" | custom-call | tf_op jit(solution)/shard_map/pallas_call | solution.py:301
  19.3 0.6 %copy.11 = bf16[2,1152]{1,0:T(2,128)(2,1)} copy(bf16[2,1152]{1,0:T(2,128)(2,1)S(1)} %shard_map.91) | data formatting | bytes 9216

commit v5 on v4

--- a/solution.py
+++ b/solution.py
@@ -315,8 +315,8 @@
             pltpu.VMEM((n, own * requests, HD), bf16),
             pltpu.VMEM((n, own * requests, HD), bf16),
             pltpu.VMEM((nb,) + queries.shape, bf16),
-            pltpu.VMEM((n, lines, columns), f32),
-            pltpu.VMEM((n, lines, columns), f32),
+            pltpu.VMEM((n, lines, columns), bf16),
+            pltpu.VMEM((n, lines, columns), bf16),
             dma((6,)),
             dma((5,)),
             dma((4,)),

time: 20.1 us -> 19.9 us (0.990)
  no operation moved by 1% of the time
where the time goes in v5:
time: 19.9 us; the launch traced here: 19.7 us
  Pallas kernels  19.1 us (96%)
  local copies, waits for them, and re-layouts  0.6 us (3%)
    pallas_call x1, Pallas kernels, on_device(): pl.pallas_call(functools.partial(kernel, n, nb), out_shape=pltpu.VMEM((li...  19.1 us
    unnamed x1, local copies, waits for them, and re-layouts  0.6 us

profile of v5, /device:TPU:0, one launch (start us, length us, event | category | flops | bytes accessed | tf_op | source)
XLA Modules:
  0.0 19.7 jit_solution(8982434061911012094)
XLA Ops:
  0.0 19.1 %shard_map.91 = bf16[2,1152]{1,0:T(2,128)(2,1)S(1)} custom-call(bf16[4,512]{1,0:T(4,128)(2,1)} %q_hbm.1, bf16[4,128,2048]{2,1,0:T(8,128)(2,1)} %k_hbm.1, bf16[4,128,2048]{2,1,0:T(8,128)(2,1)} %v_hbm.1, bf16[4,2048]{1,0:T(4,128)(2,1)} %nk_hbm.1, bf16[4,2048]{1,0:T(4,128)(2,1)} %nv_hbm.1, s32[1,4]{1,0:T(1,128)} %bitcast.3, s32[1,4]{1,0:T(1,128)} %bitcast.4, ...), custom_call_target="tpu_custom_call" | custom-call | tf_op jit(solution)/shard_map/pallas_call | solution.py:301
  19.1 0.6 %copy.11 = bf16[2,1152]{1,0:T(2,128)(2,1)} copy(bf16[2,1152]{1,0:T(2,128)(2,1)S(1)} %shard_map.91) | data formatting | bytes 9216
